TPU v7x, 128 devices: a whole 4x4x4 slice. The times are simulated.
128 devices in a mesh: occ: 4 (over x), vir: 32 (over y, z, core).
Axes of the slice: x: 4, y: 4, z: 4, core: 2. Of those that a mesh axis runs over, the one named last changes fastest.
Arguments:
- amplitudes: bfloat16 [256, 262144], P('occ', 'vir'), may hold values from -6 to 6
- cycle_integrals: bfloat16 [16, 64, 16, 64], P(None, None, 'occ'), may hold values from -0.1875 to 0.1875
- ladder_tiles: bfloat16 [2048, 4, 128, 128], P('vir'), may hold values from -0.25 to 0.25
- ladder_rows: int32 [2048, 4], P('vir'), may hold values from 0 to 2047, as said below
- ladder_count: int32 [2048], P('vir'), may hold values from 2 to 4
- row_gap: float32 [256], P('occ'), may hold values from 1 to 3
- column_energy: float32 [262144], P('vir'), may hold values from 0.5 to 8
Outputs:
- updated: bfloat16 [256, 262144], P('occ', 'vir')
Inputs may be any that keep to these rules, and one draw needn't show every extreme that they name: `ladder_rows`: each entry of column tile c's list names a virtual-pair tile within 2 tiles of c; entry 0 is max(c - 2, 0) and entry 1 is min(c + 2, 2047).
All inputs are finite; a program needn't handle non-finite values.
Results may differ from a plain program's by a relative error of at most 0.0019.
Values may be sent and summed in bfloat16 or wider, within the bound.
A program may use at most 192 MiB of HBM per device.

v0:
```python
import jax
import jax.numpy as jnp
from jax import lax
from jax.sharding import PartitionSpec as P

TILE = 128
NJ = 16
NA = 4096
NB_DEV = 2
KMAX = 4
HT = 2


def extended(block, sides, width):
    for axis, dim in sides:
        count = lax.axis_size(axis)
        forward = [(i, i + 1) for i in range(count - 1)]
        backward = [(target, source) for source, target in forward]
        low = lax.ppermute(
            lax.slice_in_dim(block, block.shape[dim] - width, None, axis=dim), axis, forward
        )
        high = lax.ppermute(lax.slice_in_dim(block, 0, width, axis=dim), axis, backward)
        block = jnp.concatenate([low, block, high], axis=dim)
    return block


def local(
    amplitudes, cycle_integrals, ladder_tiles, ladder_rows, ladder_count, row_gap, column_energy
):
    rows_dev = amplitudes.shape[0]
    cols_dev = amplitudes.shape[1]
    outer_occ = rows_dev // NJ
    four_dim = amplitudes.reshape(outer_occ, NJ, NB_DEV, NA)
    cycle_input = lax.all_to_all(four_dim, "vir", split_axis=3, concat_axis=2, tiled=True)
    tiles_dev = cols_dev // TILE
    padded = extended(amplitudes, (("vir", 1),), HT * TILE)
    own_tiles = lax.axis_index("vir") * tiles_dev + jnp.arange(tiles_dev, dtype=jnp.int32)
    relative = ladder_rows - own_tiles[:, None]
    live_mask = jnp.arange(KMAX, dtype=jnp.int32)[None, :] < ladder_count[:, None]
    ladder = jnp.zeros((rows_dev, tiles_dev, TILE), jnp.float32)
    for offset in range(2 * HT + 1):
        window = padded[:, offset * TILE : offset * TILE + cols_dev].reshape(
            rows_dev, tiles_dev, TILE
        )
        for entry in range(KMAX):
            selected = live_mask[:, entry] & (relative[:, entry] == offset - HT)
            masked = jnp.where(
                selected[:, None, None], ladder_tiles[:, entry], jnp.zeros((), jnp.bfloat16)
            )
            ladder = ladder + jnp.einsum(
                "rcp,cpq->rcq", window, masked, preferred_element_type=jnp.float32
            )
    ladder = ladder.reshape(rows_dev, cols_dev)
    all_rows = lax.all_gather(cycle_input, "occ", axis=0, tiled=True)
    cycle_part = jnp.einsum(
        "ijba,jbkc->ikca", all_rows, cycle_integrals, preferred_element_type=jnp.float32
    ).astype(jnp.bfloat16)
    cycle_pair = lax.all_to_all(
        lax.all_to_all(cycle_part, "occ", split_axis=0, concat_axis=1, tiled=True),
        "vir",
        split_axis=2,
        concat_axis=3,
        tiled=True,
    )
    cycle_flat = cycle_pair.reshape(rows_dev, cols_dev)
    denominator = row_gap[:, None] + column_energy[None, :]
    updated = (
        amplitudes.astype(jnp.float32) + (cycle_flat.astype(jnp.float32) + ladder) / denominator
    )
    return updated.astype(jnp.bfloat16)


def solution(mesh):
    in_specs = (
        P("occ", "vir"),
        P(None, None, "occ", None),
        P("vir", None, None, None),
        P("vir", None),
        P("vir"),
        P("occ"),
        P("vir"),
    )
    out_specs = P("occ", "vir")
    return jax.shard_map(local, mesh=mesh, in_specs=in_specs, out_specs=out_specs, check_vma=False)
```

profile of v0, /device:TPU:1, one launch (start us, length us, event | category | flops | bytes accessed | tf_op | source)
XLA Modules:
  0.0 195.1 jit_solution(11123908715003614297)
XLA Ops:
  6.5 0.8 fusion.152
  7.3 4.9 %collective-permute-start = (bf16[64,256]{1,0:T(8,128)(2,1)S(1)}, bf16[64,256]{1,0:T(8,128)(2,1)S(1)}, u32[]{:S(2)}, u32[]{:S(2)}) collective-permute-start(bf16[64,256]{1,0:T(8,128)(2,1)S(1)} %get-tuple-element.11), channel_id=1, source_target_pairs={{0,1},{1,2},{2,3},{3,4},{4,5},{5,6},{6,7},{7,8},{8,9},{9,10},{10,1... | collective-permute-start | bytes 98312 | tf_op jit(solution)/shard_map/ppermute | solution.py:19
  12.2 1.9 collective-permute-start.1
  14.2 1.8 reshape.294
  16.0 9.4 %copy.133 = bf16[4,16,2,4096]{1,0,2,3:T(4,128)(2,1)} copy(bf16[4,16,2,4096]{3,2,1,0:T(2,128)(2,1)S(1)} %reshape.294) | data formatting | bytes 2097152 | tf_op jit(solution)/shard_map/reshape | solution.py:33
  25.5 11.2 %reshape.306 = bf16[32,2,8192]{2,1,0:T(2,128)(2,1)} reshape(bf16[4096,2,4,16]{3,2,1,0:T(4,128)(2,1)} %bitcast.213) | data formatting | bytes 2097152
  36.7 8.4 %all-to-all-start = ((bf16[32,2,8192]{2,1,0:T(2,128)(2,1)}), bf16[32,2,8192]{2,1,0:T(2,128)(2,1)S(1)}, u32[]{:S(2)}, u32[]{:S(2)}) async-start(bf16[32,2,8192]{2,1,0:T(2,128)(2,1)} %reshape.306), calls=%async_computation | async-start | bytes 2097152 | tf_op jit(solution)/shard_map/all_to_all | solution.py:34
  45.1 0.0 all-gather.2.cloned.1.call-start
  45.2 0.0 copy-done.7
  45.2 0.0 copy-done.4
  45.3 0.0 copy-done
  45.3 3.7 %fusion.12 = f32[64,128,64]{1,2,0:T(8,128)} fusion(pred[64]{0:T(512)(128)(4,1)S(1)} %get-tuple-element.23, bf16[64,4,128,128]{3,2,1,0:T(8,128)(2,1)} %param.9, bf16[64,8192]{1,0:T(8,128)(2,1)S(1)} %copy-done), kind=kOutput, calls=%fused_computation.23 | convolution fusion | flops 135266304 | bytes 5242944 | tf_op jit(solution)/shard_map/rcp,cpq->rcq/dot_general | solution.py:50
  49.0 3.6 %fusion.17 = f32[64,128,64]{1,2,0:T(8,128)} fusion(pred[64]{0:T(512)(128)(4,1)S(1)} %get-tuple-element.15, bf16[64,4,128,128]{3,2,1,0:T(8,128)(2,1)} %param.9, bf16[64,8192]{1,0:T(8,128)(2,1)S(1)} %copy-done), kind=kOutput, calls=%fused_computation.33 | convolution fusion | flops 135266304 | bytes 5242944 | tf_op jit(solution)/shard_map/rcp,cpq->rcq/dot_general | solution.py:50
  52.7 3.7 %fusion.23 = f32[64,128,64]{1,2,0:T(8,128)} fusion(pred[64]{0:T(512)(128)(4,1)S(1)} %get-tuple-element.19, bf16[64,4,128,128]{3,2,1,0:T(8,128)(2,1)} %param.9, bf16[64,8192]{1,0:T(8,128)(2,1)S(1)} %copy-done), kind=kOutput, calls=%fused_computation.48 | convolution fusion | flops 135266304 | bytes 5242944 | tf_op jit(solution)/shard_map/rcp,cpq->rcq/dot_general | solution.py:50
  56.3 5.7 %all-to-all-done = bf16[32,2,8192]{2,1,0:T(2,128)(2,1)S(1)} async-done(((bf16[32,2,8192]{2,1,0:T(2,128)(2,1)}), bf16[32,2,8192]{2,1,0:T(2,128)(2,1)S(1)}, u32[]{:S(2)}, u32[]{:S(2)}) %all-to-all-start) | async-done | bytes 1048608 | tf_op jit(solution)/shard_map/all_to_all | solution.py:34
  62.0 7.6 %reshape.307 = bf16[4096,2,4,16]{3,2,1,0:T(4,128)(2,1)} reshape(bf16[32,2,8192]{2,1,0:T(2,128)(2,1)S(1)} %all-to-all-done) | data formatting | bytes 2097152
  69.6 12.8 %copy.134 = bf16[4,16,32,2,128]{4,3,2,1,0:T(2,128)(2,1)} copy(bf16[4,16,32,2,128]{1,0,3,4,2:T(4,128)(2,1)} %bitcast.214) | data formatting | bytes 2097152 | tf_op jit(solution)/shard_map/all_to_all | solution.py:34
  82.4 0.0 all-gather.2.cloned.1.call-update
  82.4 0.0 slice-start
  82.4 3.9 %fusion.7 = f32[64,128,64]{1,2,0:T(8,128)} fusion(pred[64]{0:T(512)(128)(4,1)S(1)} %get-tuple-element.27, bf16[64,4,128,128]{3,2,1,0:T(8,128)(2,1)} %param.9, bf16[64,8192]{1,0:T(8,128)(2,1)S(1)} %copy-done), kind=kOutput, calls=%fused_computation.13 | convolution fusion | flops 135266304 | bytes 5242944 | tf_op jit(solution)/shard_map/rcp,cpq->rcq/dot_general | solution.py:50
  86.3 0.0 collective-permute-done
  86.3 0.0 slice-start.1
  86.4 0.1 constant_dynamic-update-slice_fusion
  86.5 0.0 collective-permute-done.1
  86.5 0.4 slice_bitcast_fusion.1
  86.9 0.0 copy-start.1
  86.9 0.3 slice_bitcast_fusion.3
  87.2 0.0 copy-start.2
  87.2 0.0 slice-done
  87.2 2.2 %slice-done.1 = s8[4194304]{0:T(1024)(128)(4,1)S(1)} async-done(((s8[8388608]{0:T(1024)(128)(4,1)}), s8[4194304]{0:T(1024)(128)(4,1)S(1)}, s32[]{:S(2)}) %slice-start.1) | async-done | bytes 4194328
  89.4 2.1 %fusion.13 = f32[64,128,64]{1,2,0:T(8,128)} fusion(pred[64]{0:T(512)(128)(4,1)S(1)} %get-tuple-element.24, bf16[64,4,128,128]{3,2,1,0:T(8,128)(2,1)S(1)} %bitcast.220, bf16[8,64,8,128]{3,2,1,0:T(8,128)(2,1)S(1)} %get-tuple-element.7), kind=kOutput, calls=%fused_computation.24 | convolution fusion | flops 135266304 | bytes 5243392 | tf_op jit(solution)/shard_map/rcp,cpq->rcq/dot_general | solution.py:50
  91.5 2.1 %fusion.18 = f32[64,128,64]{1,2,0:T(8,128)} fusion(pred[64]{0:T(512)(128)(4,1)S(1)} %get-tuple-element.16, bf16[64,4,128,128]{3,2,1,0:T(8,128)(2,1)S(1)} %bitcast.220, bf16[8,64,8,128]{3,2,1,0:T(8,128)(2,1)S(1)} %get-tuple-element.7), kind=kOutput, calls=%fused_computation.34 | convolution fusion | flops 135266304 | bytes 5243392 | tf_op jit(solution)/shard_map/rcp,cpq->rcq/dot_general | solution.py:50
  93.6 2.1 %fusion.14 = f32[64,128,64]{1,2,0:T(8,128)} fusion(pred[64]{0:T(512)(128)(4,1)S(1)} %get-tuple-element.25, bf16[64,4,128,128]{3,2,1,0:T(8,128)(2,1)S(1)} %bitcast.220, bf16[8,64,8,128]{3,2,1,0:T(8,128)(2,1)S(1)} %get-tuple-element.8), kind=kOutput, calls=%fused_computation.25 | convolution fusion | flops 135266304 | bytes 5243392 | tf_op jit(solution)/shard_map/rcp,cpq->rcq/dot_general | solution.py:50
  95.7 2.1 %fusion.19 = f32[64,128,64]{1,2,0:T(8,128)} fusion(pred[64]{0:T(512)(128)(4,1)S(1)} %get-tuple-element.17, bf16[64,4,128,128]{3,2,1,0:T(8,128)(2,1)S(1)} %bitcast.220, bf16[8,64,8,128]{3,2,1,0:T(8,128)(2,1)S(1)} %get-tuple-element.8), kind=kOutput, calls=%fused_computation.35 | convolution fusion | flops 135266304 | bytes 5243392 | tf_op jit(solution)/shard_map/rcp,cpq->rcq/dot_general | solution.py:50
  97.8 2.1 %fusion.24 = f32[64,128,64]{1,2,0:T(8,128)} fusion(pred[64]{0:T(512)(128)(4,1)S(1)} %get-tuple-element.20, bf16[64,4,128,128]{3,2,1,0:T(8,128)(2,1)S(1)} %bitcast.220, bf16[8,64,8,128]{3,2,1,0:T(8,128)(2,1)S(1)} %get-tuple-element.7), kind=kOutput, calls=%fused_computation.49 | convolution fusion | flops 135266304 | bytes 5243392 | tf_op jit(solution)/shard_map/rcp,cpq->rcq/dot_general | solution.py:50
  99.9 2.1 %fusion.8 = f32[64,128,64]{1,2,0:T(8,128)} fusion(pred[64]{0:T(512)(128)(4,1)S(1)} %get-tuple-element.28, bf16[64,4,128,128]{3,2,1,0:T(8,128)(2,1)S(1)} %bitcast.220, bf16[8,64,8,128]{3,2,1,0:T(8,128)(2,1)S(1)} %get-tuple-element.7), kind=kOutput, calls=%fused_computation.14 | convolution fusion | flops 135266304 | bytes 5243392 | tf_op jit(solution)/shard_map/rcp,cpq->rcq/dot_general | solution.py:50
  102.0 0.0 copy-done.1
  102.0 2.1 %fusion.9 = f32[64,128,64]{1,2,0:T(8,128)} fusion(pred[64]{0:T(512)(128)(4,1)S(1)} %get-tuple-element.29, bf16[64,4,128,128]{3,2,1,0:T(8,128)(2,1)S(1)} %bitcast.220, bf16[8,64,8,128]{3,2,1,0:T(8,128)(2,1)S(1)} %get-tuple-element.8), kind=kOutput, calls=%fused_computation.15 | convolution fusion | flops 135266304 | bytes 5243392 | tf_op jit(solution)/shard_map/rcp,cpq->rcq/dot_general | solution.py:50
  104.1 2.1 %fusion.11 = f32[64,128,64]{1,2,0:T(8,128)} fusion(pred[64]{0:T(512)(128)(4,1)S(1)} %get-tuple-element.21, bf16[64,4,128,128]{3,2,1,0:T(8,128)(2,1)S(1)} %bitcast.220, bf16[8,64,8,128]{3,2,1,0:T(8,128)(2,1)S(1)} %get-tuple-element.6), kind=kOutput, calls=%fused_computation.22 | convolution fusion | flops 135266304 | bytes 5243392 | tf_op jit(solution)/shard_map/rcp,cpq->rcq/dot_general | solution.py:50
  106.2 2.1 %fusion.16 = f32[64,128,64]{1,2,0:T(8,128)} fusion(pred[64]{0:T(512)(128)(4,1)S(1)} %get-tuple-element.14, bf16[64,4,128,128]{3,2,1,0:T(8,128)(2,1)S(1)} %bitcast.220, bf16[8,64,8,128]{3,2,1,0:T(8,128)(2,1)S(1)} %get-tuple-element.6), kind=kOutput, calls=%fused_computation.32 | convolution fusion | flops 135266304 | bytes 5243392 | tf_op jit(solution)/shard_map/rcp,cpq->rcq/dot_general | solution.py:50
  108.3 0.0 copy-done.2
  108.3 2.0 %fusion.22 = f32[64,128,64]{1,2,0:T(8,128)} fusion(pred[64]{0:T(512)(128)(4,1)S(1)} %get-tuple-element.18, bf16[64,4,128,128]{3,2,1,0:T(8,128)(2,1)S(1)} %bitcast.220, bf16[8,64,8,128]{3,2,1,0:T(8,128)(2,1)S(1)} %get-tuple-element.6), kind=kOutput, calls=%fused_computation.47 | convolution fusion | flops 135266304 | bytes 5243392 | tf_op jit(solution)/shard_map/rcp,cpq->rcq/dot_general | solution.py:50
  110.4 2.1 %fusion.21 = f32[64,128,64]{1,2,0:T(8,128)} fusion(pred[64]{0:T(512)(128)(4,1)S(1)} %get-tuple-element.22, bf16[64,4,128,128]{3,2,1,0:T(8,128)(2,1)S(1)} %bitcast.220, bf16[8,64,8,128]{3,2,1,0:T(8,128)(2,1)S(1)} %get-tuple-element.5), kind=kOutput, calls=%fused_computation.46 | convolution fusion | flops 135266304 | bytes 5243392 | tf_op jit(solution)/shard_map/rcp,cpq->rcq/dot_general | solution.py:50
  112.5 2.0 %fusion.5 = f32[64,128,64]{1,2,0:T(8,128)} fusion(pred[64]{0:T(512)(128)(4,1)S(1)} %get-tuple-element.30, bf16[64,4,128,128]{3,2,1,0:T(8,128)(2,1)S(1)} %bitcast.220, bf16[8,64,8,128]{3,2,1,0:T(8,128)(2,1)S(1)} %get-tuple-element.5), kind=kOutput, calls=%fused_computation.11 | convolution fusion | flops 135266304 | bytes 5243392 | tf_op jit(solution)/shard_map/rcp,cpq->rcq/dot_general | solution.py:50
  114.5 13.9 %all-gather.2.cloned.1.call-done = bf16[16,16,64,128]{3,2,1,0:T(8,128)(2,1)} async-done(((bf16[4,16,64,128]{3,2,1,0:T(8,128)(2,1)}), bf16[16,16,64,128]{3,2,1,0:T(8,128)(2,1)}) %all-gather.2.cloned.1.call-update) | async-done | bytes 4194320 | tf_op jit(solution)/shard_map/all_gather | solution.py:54
  128.4 0.0 copy-done.6
  128.4 3.5 %fusion.48 = bf16[16,4,64,128]{3,2,0,1:T(8,128)(2,1)S(1)} fusion(bf16[16,16,64,128]{3,2,1,0:T(8,128)(2,1)} %all-gather.2.cloned.1.call-done, bf16[16,64,4,64,1]{3,2,1,0,4:T(4,128)(2,1)S(1)} %bitcast.221), kind=kOutput, calls=%fused_computation.72 | convolution fusion | flops 1074266112 | bytes 5767168 | tf_op jit(solution)/shard_map/ijba,jbkc->ikca/dot_general | solution.py:55
  131.8 1.0 copy.136
  132.9 3.7 %all-to-all-start.1 = ((bf16[16,4,64,128]{3,2,1,0:T(8,128)(2,1)}), bf16[16,4,64,128]{3,2,1,0:T(8,128)(2,1)S(1)}, u32[]{:S(2)}, u32[]{:S(2)}) async-start(bf16[16,4,64,128]{3,2,1,0:T(8,128)(2,1)} %copy.136), calls=%async_computation.1 | async-start | bytes 2097152 | tf_op jit(solution)/shard_map/all_to_all | solution.py:59
  136.6 4.0 %fusion.6 = f32[64,128,64]{1,2,0:T(8,128)} fusion(pred[64]{0:T(512)(128)(4,1)S(1)} %get-tuple-element.26, bf16[64,4,128,128]{3,2,1,0:T(8,128)(2,1)} %param.9, bf16[8,64,8,128]{3,2,1,0:T(8,128)(2,1)} %copy-done.2), kind=kOutput, calls=%fused_computation.12 | convolution fusion | flops 135266304 | bytes 5242944 | tf_op jit(solution)/shard_map/rcp,cpq->rcq/dot_general | solution.py:50
  140.7 3.6 %fusion.10 = f32[64,128,64]{1,2,0:T(8,128)} fusion(pred[64]{0:T(512)(128)(4,1)S(1)} %get-tuple-element.32, bf16[64,4,128,128]{3,2,1,0:T(8,128)(2,1)} %param.9, bf16[8,64,8,128]{3,2,1,0:T(8,128)(2,1)S(1)} %get-tuple-element.5), kind=kOutput, calls=%fused_computation.21 | convolution fusion | flops 135266304 | bytes 5242944 | tf_op jit(solution)/shard_map/rcp,cpq->rcq/dot_general | solution.py:50
  144.3 3.6 %fusion.15 = f32[64,128,64]{1,2,0:T(8,128)} fusion(pred[64]{0:T(512)(128)(4,1)S(1)} %get-tuple-element.31, bf16[64,4,128,128]{3,2,1,0:T(8,128)(2,1)} %param.9, bf16[8,64,8,128]{3,2,1,0:T(8,128)(2,1)S(1)} %get-tuple-element.5), kind=kOutput, calls=%fused_computation.31 | convolution fusion | flops 135266304 | bytes 5242944 | tf_op jit(solution)/shard_map/rcp,cpq->rcq/dot_general | solution.py:50
  147.9 2.9 %all-to-all-done.1 = bf16[16,4,64,128]{3,2,1,0:T(8,128)(2,1)S(1)} async-done(((bf16[16,4,64,128]{3,2,1,0:T(8,128)(2,1)}), bf16[16,4,64,128]{3,2,1,0:T(8,128)(2,1)S(1)}, u32[]{:S(2)}, u32[]{:S(2)}) %all-to-all-start.1) | async-done | bytes 1048608 | tf_op jit(solution)/shard_map/all_to_all | solution.py:59
  150.9 0.1 copy.137
  151.0 1.6 copy.138
  152.6 8.6 %all-to-all-start.2 = ((bf16[4,16,64,128]{3,1,0,2:T(8,128)(2,1)}), bf16[4,16,64,128]{3,1,0,2:T(8,128)(2,1)}, u32[]{:S(2)}, u32[]{:S(2)}) async-start(bf16[4,16,64,128]{3,1,0,2:T(8,128)(2,1)} %copy.138), calls=%async_computation.2 | async-start | bytes 2097152 | tf_op jit(solution)/shard_map/all_to_all | solution.py:58
  161.3 15.6 %fusion.20 = f32[64,8,8,128]{3,2,1,0:T(8,128)S(1)} fusion(f32[64,128,64]{1,2,0:T(8,128)} %fusion.9, f32[64,128,64]{1,2,0:T(8,128)} %fusion.14, f32[64,128,64]{1,2,0:T(8,128)} %fusion.19, f32[64,128,64]{1,2,0:T(8,128)} %fusion.8, f32[64,128,64]{1,2,0:T(8,128)} %fusion.13, f32[64,128,64]{1,2,0:T(8,128)} %fusion.24, f32[64,128,64]{1,2,0:T(8,128)} %fusion.18, ...), kind=kOutput, calls=%fused_computation.38 | convolution fusion | flops 145227776 | bytes 45088832 | tf_op jit(solution)/shard_map/rcp,cpq->rcq/dot_general | solution.py:50
  176.9 1.4 all-to-all-done.2
  178.2 1.4 copy.139
  179.6 0.3 convert_bitcast_fusion
  179.9 2.6 %copy.140 = f32[4,16,2,32,128]{4,3,2,1,0:T(8,128)} copy(f32[4,16,2,32,128]{4,1,2,3,0:T(8,128)S(1)} %convert_bitcast_fusion) | data formatting | bytes 4194304 | tf_op jit(solution)/shard_map/convert_element_type | solution.py:68
  182.5 2.7 %reshape.301 = f32[64,8192]{1,0:T(8,128)} reshape(f32[4,16,2,32,128]{4,3,2,1,0:T(8,128)} %copy.140) | data formatting | bytes 4194304 | tf_op jit(solution)/shard_map/convert_element_type | solution.py:68
  185.2 0.0 copy-done.3
  185.2 3.1 %fusion.4 = bf16[64,8192]{1,0:T(8,128)(2,1)} fusion(f32[64,8192]{1,0:T(8,128)} %reshape.301, f32[64,8,8,128]{3,2,1,0:T(8,128)S(1)} %fusion.20, bf16[64,8192]{1,0:T(8,128)(2,1)S(1)} %copy-done, f32[8192]{0:T(1024)S(1)} %copy-done.3, f32[64]{0:T(128)S(1)} %copy-done.5), kind=kLoop, calls=%fused_computation.5 | loop fusion | flops 3145728 | bytes 6324480 | tf_op jit(solution)/shard_map/convert_element_type | solution.py:70
  (16 shorter events, 0.1 us)
Async XLA Ops:
  7.3 79.0 %collective-permute-start = (bf16[64,256]{1,0:T(8,128)(2,1)S(1)}, bf16[64,256]{1,0:T(8,128)(2,1)S(1)}, u32[]{:S(2)}, u32[]{:S(2)}) collective-permute-start(bf16[64,256]{1,0:T(8,128)(2,1)S(1)} %get-tuple-element.11), channel_id=1, source_target_pairs={{0,1},{1,2},{2,3},{3,4},{4,5},{5,6},{6,7},{7,8},{8,9},{9,10},{10,1... | collective-permute-start | bytes 98312 | tf_op jit(solution)/shard_map/ppermute | solution.py:19
  12.2 74.3 %collective-permute-start.1 = (bf16[64,256]{1,0:T(8,128)(2,1)S(1)}, bf16[64,256]{1,0:T(8,128)(2,1)S(1)}, u32[]{:S(2)}, u32[]{:S(2)}) collective-permute-start(bf16[64,256]{1,0:T(8,128)(2,1)S(1)} %get-tuple-element.12), channel_id=1, source_target_pairs={{1,0},{2,1},{3,2},{4,3},{5,4},{6,5},{7,6},{8,7},{9,8},{10,9},{11,1... | collective-permute-start | bytes 98312 | tf_op jit(solution)/shard_map/ppermute | solution.py:22
  36.7 8.5 %copy-start.7 = (s32[64]{0:T(128)S(1)}, s32[64]{0:T(128)}, u32[]{:S(2)}) copy-start(s32[64]{0:T(128)} %param.11) | copy-start | bytes 772
  36.7 8.5 %copy-start.4 = (s32[64,4]{0,1:T(4,128)S(1)}, s32[64,4]{0,1:T(4,128)}, u32[]{:S(2)}) copy-start(s32[64,4]{0,1:T(4,128)} %param.10) | copy-start | bytes 3076
  36.7 8.6 %copy-start = (bf16[64,8192]{1,0:T(8,128)(2,1)S(1)}, bf16[64,8192]{1,0:T(8,128)(2,1)}, u32[]{:S(2)}) copy-start(bf16[64,8192]{1,0:T(8,128)(2,1)} %param.7) | copy-start | bytes 3145732
  36.7 25.4 %all-to-all-start = ((bf16[32,2,8192]{2,1,0:T(2,128)(2,1)}), bf16[32,2,8192]{2,1,0:T(2,128)(2,1)S(1)}, u32[]{:S(2)}, u32[]{:S(2)}) async-start(bf16[32,2,8192]{2,1,0:T(2,128)(2,1)} %reshape.306), calls=%async_computation | async-start | bytes 2097152 | tf_op jit(solution)/shard_map/all_to_all | solution.py:34
  45.1 83.3 %all-gather.2.cloned.1.call-start = ((), (), s32[]{:S(2)}) async-start(), calls=%async_computation.3 | async-start | bytes 5242880 | tf_op jit(solution)/shard_map/all_gather | solution.py:54
  82.4 4.8 %slice-start = ((s8[8388608]{0:T(1024)(128)(4,1)}), s8[4194304]{0:T(1024)(128)(4,1)S(1)}, s32[]{:S(2)}) async-start(s8[8388608]{0:T(1024)(128)(4,1)} %bitcast.219), calls=%async_computation.4 | async-start | bytes 8388608
  86.3 3.1 %slice-start.1 = ((s8[8388608]{0:T(1024)(128)(4,1)}), s8[4194304]{0:T(1024)(128)(4,1)S(1)}, s32[]{:S(2)}) async-start(s8[8388608]{0:T(1024)(128)(4,1)} %bitcast.219), calls=%async_computation.5 | async-start | bytes 8388608
  86.9 15.1 %copy-start.1 = (bf16[8,64,8,128]{3,2,1,0:T(8,128)(2,1)}, bf16[8,64,8,128]{3,2,1,0:T(8,128)(2,1)S(1)}, u32[]{:S(2)}) copy-start(bf16[8,64,8,128]{3,2,1,0:T(8,128)(2,1)S(1)} %get-tuple-element.8) | copy-start | bytes 3145732
  87.2 21.1 %copy-start.2 = (bf16[8,64,8,128]{3,2,1,0:T(8,128)(2,1)}, bf16[8,64,8,128]{3,2,1,0:T(8,128)(2,1)S(1)}, u32[]{:S(2)}) copy-start(bf16[8,64,8,128]{3,2,1,0:T(8,128)(2,1)S(1)} %get-tuple-element.6) | copy-start | bytes 3145732
  112.5 15.9 %copy-start.6 = (bf16[16,64,4,64]{3,2,1,0:T(4,128)(2,1)S(1)}, bf16[16,64,4,64]{3,2,1,0:T(4,128)(2,1)}, u32[]{:S(2)}) copy-start(bf16[16,64,4,64]{3,2,1,0:T(4,128)(2,1)} %param.8) | copy-start | bytes 1572868
  132.9 18.0 %all-to-all-start.1 = ((bf16[16,4,64,128]{3,2,1,0:T(8,128)(2,1)}), bf16[16,4,64,128]{3,2,1,0:T(8,128)(2,1)S(1)}, u32[]{:S(2)}, u32[]{:S(2)}) async-start(bf16[16,4,64,128]{3,2,1,0:T(8,128)(2,1)} %copy.136), calls=%async_computation.1 | async-start | bytes 2097152 | tf_op jit(solution)/shard_map/all_to_all | solution.py:59
  152.6 25.6 %all-to-all-start.2 = ((bf16[4,16,64,128]{3,1,0,2:T(8,128)(2,1)}), bf16[4,16,64,128]{3,1,0,2:T(8,128)(2,1)}, u32[]{:S(2)}, u32[]{:S(2)}) async-start(bf16[4,16,64,128]{3,1,0,2:T(8,128)(2,1)} %copy.138), calls=%async_computation.2 | async-start | bytes 2097152 | tf_op jit(solution)/shard_map/all_to_all | solution.py:58
  182.5 2.7 %copy-start.3 = (f32[8192]{0:T(1024)S(1)}, f32[8192]{0:T(1024)}, u32[]{:S(2)}) copy-start(f32[8192]{0:T(1024)} %param.13) | copy-start | bytes 98308
  182.5 2.7 %copy-start.5 = (f32[64]{0:T(128)S(1)}, f32[64]{0:T(128)}, u32[]{:S(2)}) copy-start(f32[64]{0:T(128)} %param.12) | copy-start | bytes 772
Sparse Core Ops, SparseCore 0:
  82.6 45.7 all-gather.1
where the time goes:
time: 196 us; the launch traced here: 195 us
  matrix products  70.3 us (36%)
  local copies, waits for them, and re-layouts  56.1 us (29%)
  starting transfers between devices  27.7 us (14%)
  waiting for transfers between devices  23.9 us (12%)
  between operations  13.7 us (7%)
  other arithmetic  3.39 us (2%)
    dot_general x20, matrix products, local(): jnp.einsum('rcp,cpq->rcq', window, masked, preferred_element_type=jnp.flo...  66.9 us
    unnamed x25, local copies, waits for them, and re-layouts  21.7 us
    all_gather x1, waiting for transfers between devices, local(): all_rows = lax.all_gather(cycle_input, 'occ', axis=0, tiled=True)  13.9 us
    all_to_all x1, local copies, waits for them, and re-layouts, local(): lax.all_to_all(four_dim, 'vir', split_axis=3, concat_axis=2, tiled=True)  12.8 us
    reshape x2, local copies, waits for them, and re-layouts, local(): four_dim = amplitudes.reshape(outer_occ, NJ, NB_DEV, NA)  11.3 us
    all_to_all x1, starting transfers between devices, local(): lax.all_to_all(lax.all_to_all(cycle_part, 'occ', split_axis=0, concat_axi...  8.64 us
    all_to_all x1, starting transfers between devices, local(): lax.all_to_all(four_dim, 'vir', split_axis=3, concat_axis=2, tiled=True)  8.45 us
    all_to_all x1, waiting for transfers between devices, local(): lax.all_to_all(four_dim, 'vir', split_axis=3, concat_axis=2, tiled=True)  5.69 us
  transfers between devices with their start and end apart: 6, of which 4 were waited for; matrix products, arithmetic and copies ran while one was open for 57% of the time, Pallas kernels for 0%

commit v1 on v0

v1 whole, which is shorter than its diff:
```python
import functools
import itertools

import jax
import jax.numpy as jnp
from jax import lax
from jax.experimental import pallas as pl
from jax.experimental.pallas import tpu as pltpu
from jax.sharding import PartitionSpec as P

TILE = 128
NJ = 16
NA = 4096
NB_DEV = 2
KMAX = 4
HT = 2
MESH = pl.DeviceIdType.MESH

STEPS = sorted(
    (d for d in itertools.product(range(4), range(4), range(2)) if any(d)),
    key=lambda d: -(min(d[0], 4 - d[0]) + min(d[1], 4 - d[1])),
)


def kernel(
    rows_ref, count_ref, amp_ref, integrals_ref, tiles_ref, gap_ref, energy_ref, out_ref,
    amp, blocks, weights, tiles, made, cycle, base, scale,
    in_send, in_recv, w_send, w_recv, f_send, f_recv, out_send, out_recv,
    halo_send, halo_recv, local_sem,
):
    occ, vir = lax.axis_index("occ"), lax.axis_index("vir")
    y, z, core = vir // 8, (vir // 2) % 4, vir % 2
    rows_dev = amp_ref.shape[0]
    cols_dev = amp_ref.shape[1]
    tiles_dev = cols_dev // TILE
    halo = HT * TILE

    def partner(d):
        return (((y + d[0]) % 4) * 4 + (z + d[1]) % 4) * 2 + (core + d[2]) % 2

    def source(d):
        return (((y + 4 - d[0]) % 4) * 4 + (z + 4 - d[1]) % 4) * 2 + (core + d[2]) % 2

    def lanes(start, size):
        return pl.ds(pl.multiple_of(start, TILE), size)

    get_amp = pltpu.make_async_copy(amp_ref, amp.at[:, pl.ds(halo, cols_dev)], local_sem.at[0])
    get_own = pltpu.make_async_copy(integrals_ref, weights.at[occ], local_sem.at[1])
    get_tiles = pltpu.make_async_copy(tiles_ref, tiles, local_sem.at[2])
    get_amp.start()
    get_own.start()

    barrier = pltpu.get_barrier_semaphore()
    for d in STEPS:
        pl.semaphore_signal(barrier, inc=1, device_id=(occ, partner(d)), device_id_type=MESH)
    for s in (2, 1, 3):
        pl.semaphore_signal(barrier, inc=1, device_id=((occ + s) % 4, vir), device_id_type=MESH)
    get_tiles.start()
    pl.semaphore_wait(barrier, len(STEPS) + 3)

    half = weights.shape[1] // 2
    mine = pl.ds(pl.multiple_of(core * half, half), half)
    w_copies = []
    get_own.wait()
    for n, s in enumerate((1, 3, 2)):
        w_copies.append(pltpu.make_async_remote_copy(
            weights.at[occ, mine], weights.at[occ, mine], w_send.at[n], w_recv.at[n],
            device_id=((occ + s) % 4, vir), device_id_type=MESH,
        ))
        w_copies[-1].start()

    own_in = []
    for b in range(NB_DEV):
        own_in.append(pltpu.make_async_copy(
            amp_ref.at[:, lanes(b * NA + vir * TILE, TILE)], blocks.at[vir, b], in_recv
        ))
        own_in[-1].start()
    for d in STEPS:
        u = partner(d)
        for b in range(NB_DEV):
            pltpu.make_async_remote_copy(
                amp_ref.at[:, lanes(b * NA + u * TILE, TILE)], blocks.at[vir, b], in_send, in_recv,
                device_id=(occ, u), device_id_type=MESH,
            ).start()

    get_amp.wait()
    up = pltpu.make_async_remote_copy(
        amp.at[:, pl.ds(cols_dev, halo)], amp.at[:, pl.ds(0, halo)], halo_send.at[0], halo_recv.at[0],
        device_id=(occ, (vir + 1) % 32), device_id_type=MESH,
    )
    down = pltpu.make_async_remote_copy(
        amp.at[:, pl.ds(halo, halo)], amp.at[:, pl.ds(halo + cols_dev, halo)], halo_send.at[1],
        halo_recv.at[1], device_id=(occ, (vir + 31) % 32), device_id_type=MESH,
    )
    up.start()
    down.start()

    gap_row = jnp.broadcast_to(gap_ref[...], (rows_dev, rows_dev))
    on_diagonal = lax.broadcasted_iota(jnp.int32, (rows_dev, rows_dev), 0) == lax.broadcasted_iota(
        jnp.int32, (rows_dev, rows_dev), 1
    )
    gap = jnp.sum(jnp.where(on_diagonal, gap_row, 0.0), axis=1, keepdims=True)
    gap = jnp.broadcast_to(gap, (rows_dev, TILE))

    up.wait()
    down.wait()
    get_tiles.wait()
    first_tile = vir * tiles_dev - HT

    def ladder_step(c, carry):
        near = [amp[:, lanes((c + q) * TILE, TILE)] for q in range(2 * HT + 1)]
        tile = vir * tiles_dev + c
        at = (jnp.maximum(tile - HT, 0) - first_tile, jnp.minimum(tile + HT, 32 * tiles_dev - 1) - first_tile)
        picked = [amp[:, lanes(a * TILE, TILE)] for a in at]
        for k in range(2, KMAX):
            offset = rows_ref[k, c] - (tile - HT)
            one = near[0]
            for q in range(1, 2 * HT + 1):
                one = jnp.where(offset == q, near[q], one)
            picked.append(jnp.where(count_ref[c] > k, one, jnp.zeros_like(one)))
        term = jnp.dot(
            jnp.concatenate(picked, axis=1), tiles[c].reshape(KMAX * TILE, TILE),
            preferred_element_type=jnp.float32,
        )
        inverse = 1.0 / (gap + energy_ref[pl.ds(c, 1), :])
        old = amp[:, lanes(halo + c * TILE, TILE)].astype(jnp.float32)
        scale[c] = inverse
        base[c] = old + term * inverse
        return carry

    lax.fori_loop(0, tiles_dev, ladder_step, 0)

    forwards = []
    for n, s in enumerate((1, 3, 2)):
        w_copies[n].wait()
        part = weights.at[(occ + 4 - s) % 4, mine]
        forwards.append(pltpu.make_async_remote_copy(
            part, part, f_send.at[n], f_recv.at[n],
            device_id=(occ, partner((0, 0, 1))), device_id_type=MESH,
        ))
        forwards[-1].start()

    pltpu.make_async_copy(blocks, blocks, in_recv).wait()

    own_out = []
    for n, s in enumerate((0, 1, 3, 2)):
        o = (occ + 4 - s) % 4
        if s:
            forwards[n - 1].wait()
        w = weights[o]
        for p in range(2):
            rhs = jnp.concatenate(
                [blocks[:, :, pl.ds(i * NJ, NJ), :].reshape(-1, TILE) for i in (2 * p, 2 * p + 1)],
                axis=1,
            )
            part = jnp.dot(w, rhs, preferred_element_type=jnp.float32)
            pair = [part[:, i * TILE:(i + 1) * TILE].reshape(32, 8, TILE) for i in range(2)]
            made[o, :, p] = jnp.concatenate(pair, axis=1).astype(jnp.bfloat16)
        own_out.append(pltpu.make_async_copy(made.at[o, vir], cycle.at[vir, o], out_recv.at[len(STEPS)]))
        own_out[-1].start()
        for q, d in enumerate(STEPS):
            u = partner(d)
            pltpu.make_async_remote_copy(
                made.at[o, u], cycle.at[vir, o], out_send, out_recv.at[q],
                device_id=(occ, u), device_id_type=MESH,
            ).start()

    low = lax.broadcasted_iota(jnp.int32, (2, 4, 8, TILE), 2) < 4
    for q, d in enumerate(STEPS + [(0, 0, 0)]):
        v = source(d)
        pltpu.make_async_copy(cycle.at[v], cycle.at[v], out_recv.at[q]).wait()
        got = cycle[v].astype(jnp.float32).reshape(2, 2, 4, 8, TILE)
        even, odd = got[:, 0], got[:, 1]
        for b in range(NB_DEV):
            if b == 0:
                term = jnp.where(low, even, pltpu.roll(odd, 4, 2))
            else:
                term = jnp.where(low, pltpu.roll(even, 4, 2), odd)
            term = jnp.transpose(term, (1, 0, 2, 3)).reshape(rows_dev, TILE)
            c = b * (NA // TILE) + v
            out_ref[:, lanes(c * TILE, TILE)] = (base[c] + term * scale[c]).astype(jnp.bfloat16)

    sent = blocks.at[pl.ds(0, len(STEPS))]
    pltpu.make_async_copy(sent, sent, in_send).wait()
    sent = cycle.at[pl.ds(0, len(STEPS))]
    pltpu.make_async_copy(sent, sent, out_send).wait()


def local(
    amplitudes, cycle_integrals, ladder_tiles, ladder_rows, ladder_count, row_gap, column_energy
):
    rows_dev, cols_dev = amplitudes.shape
    tiles_dev = cols_dev // TILE
    integrals = jnp.transpose(cycle_integrals, (3, 2, 1, 0)).reshape(256, 1024)
    bf16, f32 = jnp.bfloat16, jnp.float32
    dma = pltpu.SemaphoreType.DMA
    any_space = pl.BlockSpec(memory_space=pl.ANY)
    smem, vmem = pl.BlockSpec(memory_space=pltpu.SMEM), pl.BlockSpec(memory_space=pltpu.VMEM)
    return pl.pallas_call(
        kernel,
        out_shape=jax.ShapeDtypeStruct((rows_dev, cols_dev), bf16),
        in_specs=[smem, smem, any_space, any_space, any_space, vmem, vmem],
        out_specs=vmem,
        scratch_shapes=[
            pltpu.VMEM((rows_dev, cols_dev + 2 * HT * TILE), bf16),
            pltpu.VMEM((32, NB_DEV, rows_dev, TILE), bf16),
            pltpu.VMEM((4, 256, 1024), bf16),
            pltpu.VMEM((tiles_dev, KMAX, TILE, TILE), bf16),
            pltpu.VMEM((4, 32, 2, 16, TILE), bf16),
            pltpu.VMEM((32, 4, 2, 16, TILE), bf16),
            pltpu.VMEM((tiles_dev, rows_dev, TILE), f32),
            pltpu.VMEM((tiles_dev, rows_dev, TILE), f32),
            dma, dma, dma((3,)), dma((3,)), dma((3,)), dma((3,)), dma, dma((32,)),
            dma((2,)), dma((2,)), dma((3,)),
        ],
        compiler_params=pltpu.CompilerParams(
            collective_id=0, has_side_effects=True, vmem_limit_bytes=48 * 2**20
        ),
        name="cycle_and_ladder",
    )(
        ladder_rows.T, ladder_count, amplitudes, integrals, ladder_tiles,
        row_gap.reshape(1, rows_dev), column_energy.reshape(tiles_dev, TILE),
    )


def solution(mesh):
    in_specs = (
        P("occ", "vir"),
        P(None, None, "occ", None),
        P("vir", None, None, None),
        P("vir", None),
        P("vir"),
        P("occ"),
        P("vir"),
    )
    return jax.shard_map(
        local, mesh=mesh, in_specs=in_specs, out_specs=P("occ", "vir"), check_vma=False
    )
```

time: 196 us -> 66.6 us (0.34)
  matrix products: 70.3 us -> 0 us
  Pallas kernels: 0 us -> 48.4 us
  local copies, waits for them, and re-layouts: 56.1 us -> 18 us
  starting transfers between devices: 27.7 us -> 0 us
  waiting for transfers between devices: 23.9 us -> 0 us
  between operations: 13.7 us -> 0.08 us
  other arithmetic: 3.39 us -> 0 us
    dot_general x21 -> x0, matrix products: 70.3 us -> none  [the longest x20 66.9 us: local(): jnp.einsum('rcp,cpq->rcq', window, masked, preferred_element_type=jnp.flo...]
    pallas_call x0 -> x1, Pallas kernels: none -> 48.4 us  [local(): pl.pallas_call(kernel, out_shape=jax.ShapeDtypeStruct((rows_dev, cols_dev...]
    all_to_all x3 -> x0, starting transfers between devices: 20.8 us -> none  [the longest x1 8.64 us: local(): lax.all_to_all(lax.all_to_all(cycle_part, 'occ', split_axis=0, concat_axi...]
    unnamed x25 -> x11, local copies, waits for them, and re-layouts: 21.7 us -> 0.99 us
    all_to_all x4 -> x0, local copies, waits for them, and re-layouts: 15.9 us -> none  [the longest x1 12.8 us: local(): lax.all_to_all(four_dim, 'vir', split_axis=3, concat_axis=2, tiled=True)]
    all_gather x1 -> x0, waiting for transfers between devices: 13.9 us -> none  [local(): all_rows = lax.all_gather(cycle_input, 'occ', axis=0, tiled=True)]
    all_to_all x3 -> x0, waiting for transfers between devices: 9.99 us -> none  [the longest x1 5.69 us: local(): lax.all_to_all(four_dim, 'vir', split_axis=3, concat_axis=2, tiled=True)]
    transpose x0 -> x1, local copies, waits for them, and re-layouts: none -> 8.81 us  [local(): integrals = jnp.transpose(cycle_integrals, (3, 2, 1, 0)).reshape(256, 1024)]
  transfers between devices with their start and end apart: 6 -> 0, of which waited for: 4 -> 0; matrix products, arithmetic and copies ran while one was open for 57% -> 0% of each run, Pallas kernels for 0% -> 0%
where the time goes in v1:
time: 66.6 us; the launch traced here: 66.4 us
  Pallas kernels  48.4 us (73%)
  local copies, waits for them, and re-layouts  18 us (27%)
    pallas_call x1, Pallas kernels, local(): pl.pallas_call(kernel, out_shape=jax.ShapeDtypeStruct((rows_dev, cols_dev...  48.4 us
    transpose x1, local copies, waits for them, and re-layouts, local(): integrals = jnp.transpose(cycle_integrals, (3, 2, 1, 0)).reshape(256, 1024)  8.81 us
    reshape x1, local copies, waits for them, and re-layouts, local(): integrals = jnp.transpose(cycle_integrals, (3, 2, 1, 0)).reshape(256, 1024)  8.18 us

profile of v1, /device:TPU:1, one launch (start us, length us, event | category | flops | bytes accessed | tf_op | source)
XLA Modules:
  0.0 66.4 jit_solution(14697367572075970306)
XLA Ops:
  0.0 0.0 copy-start.1
  0.0 0.0 copy-start.4
  0.0 0.0 copy-start.3
  0.0 0.0 copy-start.2
  0.0 0.0 copy-start
  0.0 8.8 %copy.9 = bf16[64,4,64,16]{3,2,1,0:T(8,128)(2,1)} copy(bf16[64,4,64,16]{0,1,2,3:T(4,128)(2,1)} %bitcast.9) | data formatting | bytes 1048576 | tf_op jit(solution)/shard_map/transpose | solution.py:194
  8.8 8.2 %reshape.9.integrals_ref = bf16[256,1024]{1,0:T(8,128)(2,1)S(1)} reshape(bf16[64,4,64,16]{3,2,1,0:T(8,128)(2,1)} %copy.9) | data formatting | bytes 1048576 | tf_op jit(solution)/shard_map/reshape | solution.py:194
  17.0 0.0 copy-done.1
  17.0 0.0 copy-done.4
  17.0 0.0 copy-done.3
  17.1 0.0 copy-done.2
  17.1 0.0 copy-done
  17.1 48.4 %cycle_and_ladder.1 = bf16[64,8192]{1,0:T(8,128)(2,1)S(1)} custom-call(s32[4,64]{1,0:T(4,128)S(1)} %bitcast.7, s32[64]{0:T(128)S(1)} %copy-done.3, bf16[64,8192]{1,0:T(8,128)(2,1)S(1)} %copy-done, bf16[256,1024]{1,0:T(8,128)(2,1)S(1)} %reshape.9.integrals_ref, bf16[64,4,128,128]{3,2,1,0:T(8,128)(2,1)} %tiles_ref.1, f32[1,64]{1,0:T(1,128)S(1)} %bitcast.8, ...), custom_call_target="tpu_custom_call" | custom-call | tf_op jit(solution)/shard_map/cycle_and_ladder/pallas_call | solution.py:199
  65.5 1.0 %copy.11 = bf16[64,8192]{1,0:T(8,128)(2,1)} copy(bf16[64,8192]{1,0:T(8,128)(2,1)S(1)} %cycle_and_ladder.1) | data formatting | bytes 2097152
Async XLA Ops:
  0.0 17.0 %copy-start.1 = (f32[8192]{0:T(1024)S(1)}, f32[8192]{0:T(1024)}, u32[]{:S(2)}) copy-start(f32[8192]{0:T(1024)} %param.13) | copy-start | bytes 98308
  0.0 17.0 %copy-start.4 = (f32[64]{0:T(128)S(1)}, f32[64]{0:T(128)}, u32[]{:S(2)}) copy-start(f32[64]{0:T(128)} %param.12) | copy-start | bytes 772
  0.0 17.0 %copy-start.3 = (s32[64]{0:T(128)S(1)}, s32[64]{0:T(128)}, u32[]{:S(2)}) copy-start(s32[64]{0:T(128)} %count_ref.1) | copy-start | bytes 772
  0.0 17.0 %copy-start.2 = (s32[64,4]{0,1:T(4,128)S(1)}, s32[64,4]{0,1:T(4,128)}, u32[]{:S(2)}) copy-start(s32[64,4]{0,1:T(4,128)} %param.10) | copy-start | bytes 3076
  0.0 17.0 %copy-start = (bf16[64,8192]{1,0:T(8,128)(2,1)S(1)}, bf16[64,8192]{1,0:T(8,128)(2,1)}, u32[]{:S(2)}) copy-start(bf16[64,8192]{1,0:T(8,128)(2,1)} %amp_ref.1) | copy-start | bytes 3145732

commit v2 on v1

v2 whole, which is shorter than its diff:
```python
import functools
import itertools

import jax
import jax.numpy as jnp
from jax import lax
from jax.experimental import pallas as pl
from jax.experimental.pallas import tpu as pltpu
from jax.sharding import PartitionSpec as P

TILE = 128
NJ = 16
NA = 4096
NB_DEV = 2
KMAX = 4
HT = 2
MESH = pl.DeviceIdType.MESH

PARTS = 2
EARLY = 8
UNROLL = 8
TURNS = (0, 1, 3, 2)

STEPS = sorted(
    (d for d in itertools.product(range(4), range(4), range(2)) if any(d)),
    key=lambda d: -(min(d[0], 4 - d[0]) + min(d[1], 4 - d[1])),
)


def kernel(
    rows_ref, count_ref, amp_ref, integrals_ref, tiles_ref, gap_ref, energy_ref, out_ref,
    amp, blocks, weights, tiles, made, cycle, base, scale, raw, spread, gap_row, energy, rows, count,
    in_send, in_recv, w_send, w_recv, f_send, f_recv, out_send, out_recv,
    halo_send, halo_recv, local_sem,
):
    occ, vir = lax.axis_index("occ"), lax.axis_index("vir")
    y, z, core = vir // 8, (vir // 2) % 4, vir % 2
    rows_dev = amp_ref.shape[0]
    cols_dev = amp_ref.shape[1]
    tiles_dev = cols_dev // TILE
    halo = HT * TILE
    part_rows = rows_dev // PARTS

    def partner(d):
        return (((y + d[0]) % 4) * 4 + (z + d[1]) % 4) * 2 + (core + d[2]) % 2

    def source(d):
        return (((y + 4 - d[0]) % 4) * 4 + (z + 4 - d[1]) % 4) * 2 + (core + d[2]) % 2

    def lanes(start, size):
        return pl.ds(pl.multiple_of(start, TILE), size)

    get_amp = pltpu.make_async_copy(amp_ref, amp.at[:, pl.ds(halo, cols_dev)], local_sem.at[0])
    get_own = pltpu.make_async_copy(integrals_ref, raw, local_sem.at[1])
    get_tiles = pltpu.make_async_copy(tiles_ref, tiles, local_sem.at[2])
    get_small = [
        pltpu.make_async_copy(a, b, local_sem.at[3 + n])
        for n, (a, b) in enumerate(
            ((gap_ref, gap_row), (energy_ref, energy), (rows_ref, rows), (count_ref, count))
        )
    ]
    get_own.start()

    barrier = pltpu.get_barrier_semaphore()
    for d in STEPS:
        pl.semaphore_signal(barrier, inc=1, device_id=(occ, partner(d)), device_id_type=MESH)
    for s in (2, 1, 3):
        pl.semaphore_signal(barrier, inc=1, device_id=((occ + s) % 4, vir), device_id_type=MESH)
    get_amp.start()
    for g in get_small:
        g.start()
    get_tiles.start()

    get_own.wait()
    spread[...] = raw[...].astype(jnp.float32)
    nb = raw.shape[1]
    n_low = raw.shape[0] // (NJ * nb)
    group = 16
    row = lax.broadcasted_iota(jnp.int32, (nb * n_low, nb), 0)
    column = lax.broadcasted_iota(jnp.int32, (nb * n_low, nb), 1)

    def turn(g, carry):
        total = jnp.zeros((nb * n_low, group * NJ), jnp.float32)
        for j2 in range(n_low):
            one = [
                spread[pl.ds((g * group + b) * n_low + j2, NJ, stride=nb * n_low), :]
                for b in range(group)
            ]
            place = jnp.where(row == column * n_low + j2, 1.0, 0.0).astype(jnp.bfloat16)
            total += lax.dot_general(
                place, jnp.concatenate(one, axis=0).astype(jnp.bfloat16), (((1,), (1,)), ((), ())),
                preferred_element_type=jnp.float32,
            )
        weights[occ, :, lanes(g * group * NJ, group * NJ)] = total.astype(jnp.bfloat16)
        return carry

    lax.fori_loop(0, nb // group, turn, 0)
    pl.semaphore_wait(barrier, len(STEPS) + 3)

    half = weights.shape[1] // 2
    mine = pl.ds(pl.multiple_of(core * half, half), half)
    w_copies = []
    for n, s in enumerate(TURNS[1:]):
        w_copies.append(pltpu.make_async_remote_copy(
            weights.at[occ, mine], weights.at[occ, mine], w_send.at[n], w_recv.at[n],
            device_id=((occ + s) % 4, vir), device_id_type=MESH,
        ))
        w_copies[-1].start()

    for p in range(PARTS):
        some = pl.ds(p * part_rows, part_rows)
        for d in STEPS:
            u = partner(d)
            for b in range(NB_DEV):
                pltpu.make_async_remote_copy(
                    amp_ref.at[some, lanes(b * NA + u * TILE, TILE)], blocks.at[p, vir, b],
                    in_send, in_recv.at[p], device_id=(occ, u), device_id_type=MESH,
                ).start()
        for b in range(NB_DEV):
            pltpu.make_async_copy(
                amp_ref.at[some, lanes(b * NA + vir * TILE, TILE)], blocks.at[p, vir, b], in_recv.at[p]
            ).start()
        if p == 0:
            get_amp.wait()
            up = pltpu.make_async_remote_copy(
                amp.at[:, pl.ds(cols_dev, halo)], amp.at[:, pl.ds(0, halo)], halo_send.at[0],
                halo_recv.at[0], device_id=(occ, (vir + 1) % 32), device_id_type=MESH,
            )
            down = pltpu.make_async_remote_copy(
                amp.at[:, pl.ds(halo, halo)], amp.at[:, pl.ds(halo + cols_dev, halo)], halo_send.at[1],
                halo_recv.at[1], device_id=(occ, (vir + 31) % 32), device_id_type=MESH,
            )
            up.start()
            down.start()

    for g in get_small:
        g.wait()
    on_diagonal = lax.broadcasted_iota(jnp.int32, (rows_dev, rows_dev), 0) == lax.broadcasted_iota(
        jnp.int32, (rows_dev, rows_dev), 1
    )
    gaps = jnp.broadcast_to(gap_row[...], (rows_dev, rows_dev))
    gap = jnp.sum(jnp.where(on_diagonal, gaps, 0.0), axis=1, keepdims=True)
    gap = jnp.broadcast_to(gap, (rows_dev, TILE))

    up.wait()
    down.wait()
    get_tiles.wait()
    first_tile = vir * tiles_dev - HT

    def ladder_step(c, carry):
        near = [amp[:, lanes((c + q) * TILE, TILE)] for q in range(2 * HT + 1)]
        tile = vir * tiles_dev + c
        at = (jnp.maximum(tile - HT, 0) - first_tile, jnp.minimum(tile + HT, 32 * tiles_dev - 1) - first_tile)
        picked = [amp[:, lanes(a * TILE, TILE)] for a in at]
        for k in range(2, KMAX):
            offset = rows[k, c] - (tile - HT)
            one = near[0]
            for q in range(1, 2 * HT + 1):
                one = jnp.where(offset == q, near[q], one)
            picked.append(jnp.where(count[c] > k, one, jnp.zeros_like(one)))
        term = jnp.dot(
            jnp.concatenate(picked, axis=1), tiles[c].reshape(KMAX * TILE, TILE),
            preferred_element_type=jnp.float32,
        )
        inverse = 1.0 / (gap + energy[pl.ds(c, 1), :])
        old = amp[:, lanes(halo + c * TILE, TILE)].astype(jnp.float32)
        scale[c] = inverse
        base[c] = old + term * inverse
        return carry

    lax.fori_loop(0, EARLY, ladder_step, 0, unroll=UNROLL)

    forwards = []

    def forward(n):
        w_copies[n].wait()
        part = weights.at[(occ + 4 - TURNS[n + 1]) % 4, mine]
        forwards.append(pltpu.make_async_remote_copy(
            part, part, f_send.at[n], f_recv.at[n],
            device_id=(occ, partner((0, 0, 1))), device_id_type=MESH,
        ))
        forwards[-1].start()

    def product(p, n):
        w = weights[(occ + 4 - TURNS[n]) % 4]
        rhs = jnp.concatenate(
            [blocks[p, :, :, pl.ds(i * NJ, NJ), :].reshape(-1, TILE) for i in range(2)], axis=1
        )
        part = jnp.dot(w, rhs, preferred_element_type=jnp.float32)
        pair = [part[:, i * TILE:(i + 1) * TILE].reshape(32, 8, TILE) for i in range(2)]
        made[:, p, n] = jnp.concatenate(pair, axis=1).astype(jnp.bfloat16)

    def send(p, n, size):
        some = pl.ds(n, size)
        pltpu.make_async_copy(
            made.at[vir, p, some], cycle.at[vir, p, some], out_recv.at[len(STEPS)]
        ).start()
        for q, d in enumerate(STEPS):
            u = partner(d)
            pltpu.make_async_remote_copy(
                made.at[u, p, some], cycle.at[vir, p, some], out_send, out_recv.at[q],
                device_id=(occ, u), device_id_type=MESH,
            ).start()

    forward(0)
    forward(1)
    pltpu.make_async_copy(blocks.at[0], blocks.at[0], in_recv.at[0]).wait()
    product(0, 0)
    forwards[0].wait()
    product(0, 1)
    send(0, 0, 2)
    forward(2)
    pltpu.make_async_copy(blocks.at[1], blocks.at[1], in_recv.at[1]).wait()
    product(1, 0)
    product(1, 1)
    send(1, 0, 2)
    forwards[1].wait()
    forwards[2].wait()
    for p in range(PARTS):
        product(p, 2)
        product(p, 3)
        send(p, 2, 2)

    lax.fori_loop(EARLY, tiles_dev, ladder_step, 0, unroll=UNROLL)

    low = lax.broadcasted_iota(jnp.int32, (4, 8, TILE), 1) < 4
    places = []
    for o in range(4):
        s = (occ + 4 - o) % 4
        places.append(s + (s // 2) * (5 - 2 * s))
    for q, d in enumerate(STEPS + [(0, 0, 0)]):
        v = source(d)
        pltpu.make_async_copy(cycle.at[v], cycle.at[v], out_recv.at[q]).wait()
        got = [cycle[v, :, n].astype(jnp.float32).reshape(4, 8, TILE) for n in places]
        for b in range(NB_DEV):
            term = []
            for even, odd in ((got[0], got[1]), (got[2], got[3])):
                if b == 0:
                    term.append(jnp.where(low, even, pltpu.roll(odd, 4, 1)))
                else:
                    term.append(jnp.where(low, pltpu.roll(even, 4, 1), odd))
            term = jnp.stack(term, axis=1).reshape(rows_dev, TILE)
            c = b * (NA // TILE) + v
            out_ref[:, lanes(c * TILE, TILE)] = (base[c] + term * scale[c]).astype(jnp.bfloat16)

    sent = blocks.at[:, pl.ds(0, len(STEPS))]
    pltpu.make_async_copy(sent, sent, in_send).wait()
    sent = cycle.at[pl.ds(0, len(STEPS))]
    pltpu.make_async_copy(sent, sent, out_send).wait()


def local(
    amplitudes, cycle_integrals, ladder_tiles, ladder_rows, ladder_count, row_gap, column_energy
):
    rows_dev, cols_dev = amplitudes.shape
    tiles_dev = cols_dev // TILE
    integrals = cycle_integrals.reshape(-1, cycle_integrals.shape[-1])
    bf16, f32 = jnp.bfloat16, jnp.float32
    dma = pltpu.SemaphoreType.DMA
    hbm, vmem = pl.BlockSpec(memory_space=pltpu.HBM), pl.BlockSpec(memory_space=pltpu.VMEM)
    return pl.pallas_call(
        kernel,
        out_shape=jax.ShapeDtypeStruct((rows_dev, cols_dev), bf16),
        in_specs=[hbm] * 7,
        out_specs=vmem,
        scratch_shapes=[
            pltpu.VMEM((rows_dev, cols_dev + 2 * HT * TILE), bf16),
            pltpu.VMEM((PARTS, 32, NB_DEV, rows_dev // PARTS, TILE), bf16),
            pltpu.VMEM((4, 256, 1024), bf16),
            pltpu.VMEM((tiles_dev, KMAX, TILE, TILE), bf16),
            pltpu.VMEM((32, PARTS, 4, 16, TILE), bf16),
            pltpu.VMEM((32, PARTS, 4, 16, TILE), bf16),
            pltpu.VMEM((tiles_dev, rows_dev, TILE), f32),
            pltpu.VMEM((tiles_dev, rows_dev, TILE), f32),
            pltpu.VMEM(integrals.shape, bf16),
            pltpu.VMEM(integrals.shape, f32),
            pltpu.VMEM((1, rows_dev), f32),
            pltpu.VMEM((tiles_dev, TILE), f32),
            pltpu.SMEM((KMAX, tiles_dev), jnp.int32),
            pltpu.SMEM((tiles_dev,), jnp.int32),
            dma, dma((PARTS,)), dma((3,)), dma((3,)), dma((3,)), dma((3,)), dma, dma((32,)),
            dma((2,)), dma((2,)), dma((7,)),
        ],
        compiler_params=pltpu.CompilerParams(
            collective_id=0, has_side_effects=True, vmem_limit_bytes=62 * 2**20
        ),
        name="cycle_and_ladder",
    )(
        ladder_rows.T, ladder_count, amplitudes, integrals, ladder_tiles,
        row_gap.reshape(1, rows_dev), column_energy.reshape(tiles_dev, TILE),
    )


def solution(mesh):
    in_specs = (
        P("occ", "vir"),
        P(None, None, "occ", None),
        P("vir", None, None, None),
        P("vir", None),
        P("vir"),
        P("occ"),
        P("vir"),
    )
    return jax.shard_map(
        local, mesh=mesh, in_specs=in_specs, out_specs=P("occ", "vir"), check_vma=False
    )
```

time: 66.6 us -> 40.7 us (0.61)
  local copies, waits for them, and re-layouts: 18 us -> 2.26 us
  Pallas kernels: 48.4 us -> 38.3 us
    pallas_call x1, Pallas kernels: 48.4 us -> 38.3 us  [local(): pl.pallas_call(kernel, out_shape=jax.ShapeDtypeStruct((rows_dev, cols_dev...]
    transpose x1 -> x0, local copies, waits for them, and re-layouts: 8.81 us -> none  [local(): integrals = jnp.transpose(cycle_integrals, (3, 2, 1, 0)).reshape(256, 1024)]
    reshape x1 -> x0, local copies, waits for them, and re-layouts: 8.18 us -> none  [local(): integrals = jnp.transpose(cycle_integrals, (3, 2, 1, 0)).reshape(256, 1024)]
    unnamed x11 -> x1, local copies, waits for them, and re-layouts: 0.99 us -> 2.26 us
where the time goes in v2:
time: 40.7 us; the launch traced here: 40.6 us
  Pallas kernels  38.3 us (94%)
  local copies, waits for them, and re-layouts  2.26 us (6%)
    pallas_call x1, Pallas kernels, local(): pl.pallas_call(kernel, out_shape=jax.ShapeDtypeStruct((rows_dev, cols_dev...  38.3 us
    unnamed x1, local copies, waits for them, and re-layouts  2.26 us

profile of v2, /device:TPU:1, one launch (start us, length us, event | category | flops | bytes accessed | tf_op | source)
XLA Modules:
  0.0 40.6 jit_solution(5952838307737134035)
XLA Ops:
  0.0 38.3 %cycle_and_ladder.1 = bf16[64,8192]{1,0:T(8,128)(2,1)} custom-call(s32[4,64]{1,0:T(4,128)} %bitcast.6, s32[64]{0:T(128)} %count_ref.1, bf16[64,8192]{1,0:T(8,128)(2,1)} %amp_ref.1, bf16[4096,64]{1,0:T(8,128)(2,1)} %bitcast.4, bf16[64,4,128,128]{3,2,1,0:T(8,128)(2,1)} %tiles_ref.1, f32[1,64]{1,0:T(1,128)} %bitcast.7, f32[64,128]{1,0:T(8,128)} %bitcast.5), custom_call_target="tpu_custom_call" | custom-call | tf_op jit(solution)/shard_map/cycle_and_ladder/pallas_call | solution.py:261
  38.3 2.3 %copy.9 = bf16[64,8192]{1,0:T(8,128)(2,1)} copy(bf16[64,8192]{1,0:T(8,128)(2,1)} %cycle_and_ladder.1) | data formatting | bytes 2097152

commit v3 on v2

--- a/solution.py
+++ b/solution.py
@@ -17,7 +17,8 @@
 MESH = pl.DeviceIdType.MESH
 
 PARTS = 2
-EARLY = 8
+EARLY = 0
+MIDDLE = 0
 UNROLL = 8
 TURNS = (0, 1, 3, 2)
 
@@ -29,7 +30,7 @@
 
 def kernel(
     rows_ref, count_ref, amp_ref, integrals_ref, tiles_ref, gap_ref, energy_ref, out_ref,
-    amp, blocks, weights, tiles, made, cycle, base, scale, raw, spread, gap_row, energy, rows, count,
+    amp, blocks, weights, tiles, made, cycle, base, scale, raw, spread, gap_row, energy, rows, count, result,
     in_send, in_recv, w_send, w_recv, f_send, f_recv, out_send, out_recv,
     halo_send, halo_recv, local_sem,
 ):
@@ -99,21 +100,28 @@
 
     half = weights.shape[1] // 2
     mine = pl.ds(pl.multiple_of(core * half, half), half)
-    w_copies = []
-    for n, s in enumerate(TURNS[1:]):
-        w_copies.append(pltpu.make_async_remote_copy(
-            weights.at[occ, mine], weights.at[occ, mine], w_send.at[n], w_recv.at[n],
-            device_id=((occ + s) % 4, vir), device_id_type=MESH,
-        ))
-        w_copies[-1].start()
-
+    quarter = half // 2
+    quarters = [pl.ds(pl.multiple_of(core * half + n * quarter, quarter), quarter) for n in range(2)]
+    after, before, across = (occ + 1) % 4, (occ + 3) % 4, (occ + 2) % 4
+
+    def along(slot, some, n, to):
+        part = weights.at[slot, some]
+        return pltpu.make_async_remote_copy(
+            part, part, w_send.at[n], w_recv.at[n], device_id=(to, vir), device_id_type=MESH
+        )
+
+    w_copies = [along(occ, mine, 0, after), along(occ, mine, 1, before)]
+    for w_copy in w_copies:
+        w_copy.start()
+
+    get_amp.wait()
     for p in range(PARTS):
         some = pl.ds(p * part_rows, part_rows)
         for d in STEPS:
             u = partner(d)
             for b in range(NB_DEV):
                 pltpu.make_async_remote_copy(
-                    amp_ref.at[some, lanes(b * NA + u * TILE, TILE)], blocks.at[p, vir, b],
+                    amp.at[some, lanes(halo + b * NA + u * TILE, TILE)], blocks.at[p, vir, b],
                     in_send, in_recv.at[p], device_id=(occ, u), device_id_type=MESH,
                 ).start()
         for b in range(NB_DEV):
@@ -121,7 +129,6 @@
                 amp_ref.at[some, lanes(b * NA + vir * TILE, TILE)], blocks.at[p, vir, b], in_recv.at[p]
             ).start()
         if p == 0:
-            get_amp.wait()
             up = pltpu.make_async_remote_copy(
                 amp.at[:, pl.ds(cols_dev, halo)], amp.at[:, pl.ds(0, halo)], halo_send.at[0],
                 halo_recv.at[0], device_id=(occ, (vir + 1) % 32), device_id_type=MESH,
@@ -170,16 +177,14 @@
 
     lax.fori_loop(0, EARLY, ladder_step, 0, unroll=UNROLL)
 
-    forwards = []
-
-    def forward(n):
-        w_copies[n].wait()
-        part = weights.at[(occ + 4 - TURNS[n + 1]) % 4, mine]
-        forwards.append(pltpu.make_async_remote_copy(
+    def forward(n, slot):
+        part = weights.at[slot, mine]
+        copy = pltpu.make_async_remote_copy(
             part, part, f_send.at[n], f_recv.at[n],
             device_id=(occ, partner((0, 0, 1))), device_id_type=MESH,
-        ))
-        forwards[-1].start()
+        )
+        copy.start()
+        return copy
 
     def product(p, n):
         w = weights[(occ + 4 - TURNS[n]) % 4]
@@ -202,14 +207,22 @@
                 device_id=(occ, u), device_id_type=MESH,
             ).start()
 
-    forward(0)
-    forward(1)
+    w_copies[0].wait()
+    w_copies.append(along(before, quarters[0], 2, after))
+    w_copies[2].start()
+    w_copies[1].wait()
+    w_copies.append(along(after, quarters[1], 3, before))
+    w_copies[3].start()
+    forwards = [forward(0, before), forward(1, after)]
     pltpu.make_async_copy(blocks.at[0], blocks.at[0], in_recv.at[0]).wait()
     product(0, 0)
     forwards[0].wait()
     product(0, 1)
     send(0, 0, 2)
-    forward(2)
+    w_copies[2].wait()
+    w_copies[3].wait()
+    forwards.append(forward(2, across))
+    lax.fori_loop(EARLY, EARLY + MIDDLE, ladder_step, 0, unroll=UNROLL)
     pltpu.make_async_copy(blocks.at[1], blocks.at[1], in_recv.at[1]).wait()
     product(1, 0)
     product(1, 1)
@@ -221,7 +234,7 @@
         product(p, 3)
         send(p, 2, 2)
 
-    lax.fori_loop(EARLY, tiles_dev, ladder_step, 0, unroll=UNROLL)
+    lax.fori_loop(EARLY + MIDDLE, tiles_dev, ladder_step, 0, unroll=UNROLL)
 
     low = lax.broadcasted_iota(jnp.int32, (4, 8, TILE), 1) < 4
     places = []
@@ -241,8 +254,11 @@
                     term.append(jnp.where(low, pltpu.roll(even, 4, 1), odd))
             term = jnp.stack(term, axis=1).reshape(rows_dev, TILE)
             c = b * (NA // TILE) + v
-            out_ref[:, lanes(c * TILE, TILE)] = (base[c] + term * scale[c]).astype(jnp.bfloat16)
-
+            at = lanes(c * TILE, TILE)
+            result[:, at] = (base[c] + term * scale[c]).astype(jnp.bfloat16)
+            pltpu.make_async_copy(result.at[:, at], out_ref.at[:, at], local_sem.at[7]).start()
+
+    pltpu.make_async_copy(result, out_ref, local_sem.at[7]).wait()
     sent = blocks.at[:, pl.ds(0, len(STEPS))]
     pltpu.make_async_copy(sent, sent, in_send).wait()
     sent = cycle.at[pl.ds(0, len(STEPS))]
@@ -257,12 +273,12 @@
     integrals = cycle_integrals.reshape(-1, cycle_integrals.shape[-1])
     bf16, f32 = jnp.bfloat16, jnp.float32
     dma = pltpu.SemaphoreType.DMA
-    hbm, vmem = pl.BlockSpec(memory_space=pltpu.HBM), pl.BlockSpec(memory_space=pltpu.VMEM)
+    hbm = pl.BlockSpec(memory_space=pltpu.HBM)
     return pl.pallas_call(
         kernel,
         out_shape=jax.ShapeDtypeStruct((rows_dev, cols_dev), bf16),
         in_specs=[hbm] * 7,
-        out_specs=vmem,
+        out_specs=hbm,
         scratch_shapes=[
             pltpu.VMEM((rows_dev, cols_dev + 2 * HT * TILE), bf16),
             pltpu.VMEM((PARTS, 32, NB_DEV, rows_dev // PARTS, TILE), bf16),
@@ -278,8 +294,9 @@
             pltpu.VMEM((tiles_dev, TILE), f32),
             pltpu.SMEM((KMAX, tiles_dev), jnp.int32),
             pltpu.SMEM((tiles_dev,), jnp.int32),
-            dma, dma((PARTS,)), dma((3,)), dma((3,)), dma((3,)), dma((3,)), dma, dma((32,)),
-            dma((2,)), dma((2,)), dma((7,)),
+            pltpu.VMEM((rows_dev, cols_dev), bf16),
+            dma, dma((PARTS,)), dma((4,)), dma((4,)), dma((3,)), dma((3,)), dma, dma((32,)),
+            dma((2,)), dma((2,)), dma((8,)),
         ],
         compiler_params=pltpu.CompilerParams(
             collective_id=0, has_side_effects=True, vmem_limit_bytes=62 * 2**20

time: 40.7 us -> 40.5 us (level)
  no operation moved by 1% of the time
where the time goes in v3:
time: 40.5 us; the launch traced here: 40.3 us
  Pallas kernels  38.1 us (94%)
  local copies, waits for them, and re-layouts  2.26 us (6%)
    pallas_call x1, Pallas kernels, local(): pl.pallas_call(kernel, out_shape=jax.ShapeDtypeStruct((rows_dev, cols_dev...  38.1 us
    unnamed x1, local copies, waits for them, and re-layouts  2.26 us

profile of v3, /device:TPU:1, one launch (start us, length us, event | category | flops | bytes accessed | tf_op | source)
XLA Modules:
  0.0 40.3 jit_solution(5174192666400274354)
XLA Ops:
  0.0 38.1 %cycle_and_ladder.1 = bf16[64,8192]{1,0:T(8,128)(2,1)} custom-call(s32[4,64]{1,0:T(4,128)} %bitcast.6, s32[64]{0:T(128)} %count_ref.1, bf16[64,8192]{1,0:T(8,128)(2,1)} %amp_ref.1, bf16[4096,64]{1,0:T(8,128)(2,1)} %bitcast.4, bf16[64,4,128,128]{3,2,1,0:T(8,128)(2,1)} %tiles_ref.1, f32[1,64]{1,0:T(1,128)} %bitcast.7, f32[64,128]{1,0:T(8,128)} %bitcast.5), custom_call_target="tpu_custom_call" | custom-call | tf_op jit(solution)/shard_map/cycle_and_ladder/pallas_call | solution.py:277
  38.1 2.3 %copy.9 = bf16[64,8192]{1,0:T(8,128)(2,1)} copy(bf16[64,8192]{1,0:T(8,128)(2,1)} %cycle_and_ladder.1) | data formatting | bytes 2097152
